TPU v7x, 512 devices: a whole 4x4x16 slice. The times are simulated.
512 devices in a mesh: grp: 32 (over y, z_lo), tp: 16 (over z_hi, x, core).
Axes of the slice: x: 4, y: 4, z: 16 (z_hi: 2, z_lo: 8; z = z_hi * 8 + z_lo), core: 2. Of those that a mesh axis runs over, the one named last changes fastest.
Arguments:
- tokens: bfloat16 [65536, 1536], P(('grp', 'tp')), may hold values from -6 to 6
- attn_gain: float32 [1536], replicated, may hold values from 0.1 to 1.9
- ffn_gain: float32 [1536], replicated, may hold values from 0.1 to 1.9
- w_query: bfloat16 [1536, 1024], P(None, 'tp')
- key_value_weight: bfloat16 [1536, 1024], P(None, 'tp'), may hold values from -0.15625 to 0.15625
- w_out: bfloat16 [1024, 1536], P('tp'), may hold values from -0.1875 to 0.1875
- segment_ids: int32 [65536], P(('grp', 'tp')), may hold values from 0 to 65535, as said below
- expert_ids: int32 [65536, 2], P(('grp', 'tp')), may hold values from 0 to 7, all different within a row; in each aligned block of 128 rows (0 to 127, 128 to 255, ...) at most 48 rows name the same one
- route_weights: float32 [65536, 2], P(('grp', 'tp')), may hold values from 0.2 to 1
- w_gate: bfloat16 [1536, 4096], P(None, 'tp'), may hold values from -0.15625 to 0.15625
- w_up: bfloat16 [1536, 4096], P(None, 'tp'), may hold values from -0.15625 to 0.15625
- w_down: bfloat16 [4096, 1536], P('tp'), may hold values from -0.25 to 0.25
- page_table: int32 [32, 128], P('grp'), may hold values from 0 to 127, each once within a row
Outputs:
- hidden_out: bfloat16 [65536, 1536], P(('grp', 'tp'))
- kv_cache: bfloat16 [4096, 16, 1024], P(('grp', 'tp'))
Inputs may be any that keep to these rules, and one draw needn't show every extreme that they name: `segment_ids`: each token's number is the stream position of its prompt's first token, so numbers never fall along the stream; a prompt covers at most 1024 tokens and some prompt exactly 1024; a prompt runs from every group into the next; the last token of the stream is a prompt of its own. `expert_ids`: in the tokens of one device no expert is named more than 48 times; in some device's tokens one expert is named exactly 48 times. `page_table`: each row names every page of the group once.
All inputs are finite; a program needn't handle non-finite values.
Results may differ from a plain program's by a relative error of at most 0.015.
The roundings to bfloat16 on the way count: a program that leaves them out, or rounds other values in their place, can miss the bound.
Values may be sent and summed in bfloat16 or wider, within the bound.
No kernel may reach another device: no remote copies, remote signals or barrier semaphores. Data moves between devices by JAX's collectives and lax.ppermute only.
A program may use at most 64 MiB of HBM per device.

v0:
```python
import functools
import jax
import jax.numpy as jnp
import numpy as np
from jax import lax
from jax.sharding import Mesh
from jax.sharding import PartitionSpec as P

AXES = ("y", "zl", "zh", "x", "c")
SIZES = (4, 8, 2, 4, 2)
ROW = ("x", "c")
PAGE = 16
CAP = 48


def permute(block, target):
    route = []
    for source in range(int(np.prod(SIZES))):
        place = dict(zip(AXES, (int(v) for v in np.unravel_index(source, SIZES))))
        goal = target(**place)
        if goal is not None:
            route.append((source, int(np.ravel_multi_index(goal, SIZES))))
    return lax.ppermute(block, AXES, route)


def swap_core(block):
    return permute(block, lambda y, zl, zh, x, c: (y, zl, zh, x, 1 - c))


def swap_half(block):
    return permute(block, lambda y, zl, zh, x, c: (y, zl, 1 - zh, x, c))


def swap_near(block):
    return permute(block, lambda y, zl, zh, x, c: (y, zl ^ 1, zh, x, c))


def next_group(block):

    def target(y, zl, zh, x, c):
        g = y * 8 + zl + 1
        return (g // 8, g % 8, zh, x, c) if zh == 0 and g < 32 else None

    return permute(block, target)


def ahead_x(block, step):
    return permute(block, lambda y, zl, zh, x, c: (y, zl, zh, (x - step) % 4, c))


def ahead_y(block, step):
    return permute(block, lambda y, zl, zh, x, c: ((y - step) % 4, zl, zh, x, c))


def from_all(block, ahead):
    one, three, two = [ahead(block, step) for step in (1, 3, 2)]
    return jnp.stack([block, one, two, three])


def in_order(relative, me):
    twice = jnp.concatenate([relative, relative], axis=0)
    return lax.dynamic_slice_in_dim(twice, (4 - me) % 4, 4, 0)


def rms_scale(row_data, gain_vec):
    values = row_data.astype(jnp.float32)
    inverse = lax.rsqrt(jnp.mean(values * values, axis=-1, keepdims=True) + 1e-05)
    return (values * inverse * gain_vec).astype(jnp.bfloat16)


def attend(queries, key_cat, value_cat, first_key, block_rows):
    rows = queries.shape[1]
    span = rows + block_rows
    outs = []
    for block in range(rows // block_rows):
        low = block * block_rows
        query = queries[:, low : low + block_rows]
        keys = key_cat[low : low + span]
        values = value_cat[low : low + span]
        position = low + jnp.arange(span, dtype=jnp.int32)
        own = rows + low + jnp.arange(block_rows, dtype=jnp.int32)
        allowed = (position[None, :] >= first_key[low : low + block_rows, None]) & (
            position[None, :] <= own[:, None]
        )
        scores = jnp.einsum("hqd,kd->hqk", query, keys, preferred_element_type=jnp.float32)
        scores = jnp.where(allowed[None], scores * 0.125, -1e30)
        exponent = jnp.exp(scores - jnp.max(scores, axis=-1, keepdims=True))
        weights = (exponent / jnp.sum(exponent, axis=-1, keepdims=True)).astype(jnp.bfloat16)
        result = jnp.einsum("hqk,kd->qhd", weights, values, preferred_element_type=jnp.float32)
        outs.append(result.astype(jnp.bfloat16).reshape(block_rows, -1))
    return jnp.concatenate(outs, axis=0)


def body(
    tokens,
    attn_gain,
    ffn_gain,
    w_query,
    key_value_weight,
    w_out,
    segment_ids,
    expert_ids,
    route_weights,
    w_gate,
    w_up,
    w_down,
    page_table,
):
    y, zl, zh, x, c = (lax.axis_index(name) for name in AXES)
    width = tokens.shape[1]
    tok = tokens.shape[0]
    rows = 8 * tok
    own_pack = jnp.concatenate([w_query.T, key_value_weight.T, w_out], axis=0)
    part = own_pack.shape[0] // 4
    far_part = swap_half(lax.dynamic_slice_in_dim(own_pack, y * part, part, 0))
    far_pack = in_order(from_all(far_part, ahead_y), y).reshape(-1, width)
    own_cols, far_cols = (own_pack[:128], far_pack[:128])
    other_own = swap_core(own_cols)
    other_far = swap_core(far_cols)
    normed_in = rms_scale(tokens, attn_gain)
    near = from_all(normed_in, ahead_x).reshape(4 * tok, width)

    def project(cols):
        return lax.dot_general(
            near, cols, (((1,), (1,)), ((), ())), preferred_element_type=jnp.float32
        ).astype(jnp.bfloat16)

    keep = jnp.concatenate([project(own_cols), project(far_cols)], axis=1)
    give = jnp.concatenate([project(other_own), project(other_far)], axis=1)
    got = swap_core(give)
    both = jnp.where(c == 0, jnp.stack([keep, got]), jnp.stack([got, keep]))
    both = both.reshape(2, 4, tok, 256).transpose(1, 0, 2, 3)
    projected = in_order(both, x).reshape(rows, 256)
    queries = jnp.stack([projected[:, 0:64], projected[:, 128:192]])
    own_kv, far_kv = (projected[:, 64:128], projected[:, 192:256])
    key_rows = jnp.where(zh == 0, own_kv, far_kv)
    value_rows = jnp.where(zh == 0, far_kv, own_kv)
    key_value = jnp.concatenate([key_rows, value_rows], axis=1)
    partner = swap_half(key_value)
    shifted = next_group(partner)
    before = jnp.where(zh == 0, shifted, partner)
    seg_near = from_all(segment_ids, ahead_x)
    seg_got = swap_core(seg_near)
    seg = jnp.where(c == 0, jnp.stack([seg_near, seg_got]), jnp.stack([seg_got, seg_near]))
    seg = in_order(seg.transpose(1, 0, 2), x).reshape(rows)
    base = ((y * 8 + zl) * 2 + zh) * rows
    first_key = seg - base + rows
    key_cat = jnp.concatenate([before[:, :64], key_rows], axis=0)
    value_cat = jnp.concatenate([before[:, 64:], value_rows], axis=0)
    attended = attend(queries, key_cat, value_cat, first_key, 512)
    group_kv = jnp.where(zh == 0, jnp.stack([key_value, partner]), jnp.stack([partner, key_value]))
    page_order = page_table[0]
    page_ids = zh * 64 + jnp.arange(64, dtype=jnp.int32)
    block_ids = jnp.arange(128, dtype=jnp.int32)
    source_block = jnp.sum(
        jnp.where(page_order[None, :] == page_ids[:, None], block_ids[None, :], 0), axis=1
    )
    pages = group_kv.reshape(128, PAGE, 128)[source_block]
    joined = jnp.concatenate([attended.reshape(8, tok, 128), pages.reshape(8, tok, 128)], axis=1)
    joined = lax.all_to_all(joined, ROW, split_axis=0, concat_axis=0, tiled=True)
    token_heads = joined[:, :tok].transpose(1, 0, 2).reshape(tok, 1024)
    kv_cache = joined[:, tok:].reshape(8, 8, PAGE, 2, 64).transpose(1, 2, 3, 0, 4)
    kv_cache = kv_cache.reshape(8, PAGE, 1024)
    out_rows = jnp.concatenate([own_pack[128:], far_pack[128:]], axis=0)
    out_all = lax.all_gather(out_rows, ROW, axis=0, tiled=True)
    out_sum = jnp.dot(token_heads, out_all, preferred_element_type=jnp.float32)
    mid_state = (tokens.astype(jnp.float32) + out_sum).astype(jnp.bfloat16)
    normed_mid = rms_scale(mid_state, ffn_gain)
    gate_up = jnp.concatenate([w_gate, w_up], axis=1)
    piece = y * 2 + zl % 2

    def far_weight(own):
        step = own.shape[0] // 8
        eighth = swap_half(lax.dynamic_slice_in_dim(own, piece * step, step, 0))
        beside = swap_near(eighth)
        pair = jnp.where(
            zl % 2 == 0,
            jnp.concatenate([eighth, beside], axis=0),
            jnp.concatenate([beside, eighth], axis=0),
        )
        return lax.all_gather(pair, "y", axis=0, tiled=True)

    def whole(own):
        far = far_weight(own)
        mine = c == zh
        kept = jnp.where(mine, own, far)
        return (kept, swap_core(jnp.where(mine, far, own)))

    gate_up_a, gate_up_b = whole(gate_up)
    down_a, down_b = whole(w_down)
    flat = expert_ids.reshape(-1)
    onehot = (flat[:, None] == jnp.arange(8, dtype=jnp.int32)[None, :]).astype(jnp.int32)
    earlier = jnp.cumsum(onehot, axis=0) - onehot
    slot = jnp.sum(earlier * onehot, axis=-1)
    holder = flat % 4 * 2 + flat // 4
    target_slot = (holder * CAP + slot).reshape(tok, 2)
    slots = jnp.arange(8 * CAP, dtype=jnp.int32)
    pick = [(target_slot[:, k : k + 1] == slots[None, :]).astype(jnp.bfloat16) for k in range(2)]
    send = lax.dot_general(
        pick[0] + pick[1], normed_mid, (((0,), (0,)), ((), ())), preferred_element_type=jnp.float32
    ).astype(jnp.bfloat16)
    arrived = lax.all_to_all(
        send.reshape(8, CAP, width), ROW, split_axis=0, concat_axis=0, tiled=True
    ).reshape(8 * CAP, width)

    def half(gate_up_half, down_half):
        both_act = jnp.dot(arrived, gate_up_half, preferred_element_type=jnp.float32)
        gate_act, up_act = (both_act[:, :256], both_act[:, 256:])
        activated = (jax.nn.silu(gate_act) * up_act).astype(jnp.bfloat16)
        return jnp.dot(activated, down_half, preferred_element_type=jnp.float32)

    expert_out = (half(gate_up_a, down_a) + half(gate_up_b, down_b)).astype(jnp.bfloat16)
    returned = lax.all_to_all(
        expert_out.reshape(8, CAP, width), ROW, split_axis=0, concat_axis=0, tiled=True
    ).reshape(8 * CAP, width)
    total = mid_state.astype(jnp.float32)
    for k in range(2):
        chosen = jnp.dot(pick[k], returned, preferred_element_type=jnp.float32)
        total = total + chosen * route_weights[:, k : k + 1]
    return (total.astype(jnp.bfloat16), kv_cache)


def solution(mesh):
    fine = Mesh(mesh.devices.reshape(SIZES), AXES)
    grp, tp = (("y", "zl"), ("zh", "x", "c"))
    in_specs = (
        P(AXES, None),
        P(),
        P(),
        P(None, tp),
        P(None, tp),
        P(tp, None),
        P(AXES),
        P(AXES, None),
        P(AXES, None),
        P(None, tp),
        P(None, tp),
        P(tp, None),
        P(grp, None),
    )
    out_specs = (P(AXES, None), P(AXES, None, None))
    return jax.shard_map(body, mesh=fine, in_specs=in_specs, out_specs=out_specs, check_vma=False)
```

profile of v0, /device:TPU:40, one launch (start us, length us, event | category | flops | bytes accessed | tf_op | source)
XLA Modules:
  0.0 277.2 jit_solution(10554161021707727774)
XLA Ops:
  8.5 2.0 fusion.30
  10.4 4.7 %collective-permute-start = (bf16[128,1536]{1,0:T(8,128)(2,1)}, bf16[128,1536]{1,0:T(8,128)(2,1)}, u32[]{:S(2)}, u32[]{:S(2)}) collective-permute-start(bf16[128,1536]{1,0:T(8,128)(2,1)} %fusion.30), channel_id=1, source_target_pairs={{0,6},{1,7},{2,0},{3,1},{4,2},{5,3},{6,4},{7,5},{8,14},{9,15},{10,... | collective-permute-start | bytes 1179656 | tf_op jit(solution)/shard_map/ppermute | solution.py:23
  15.1 2.7 collective-permute-start.1
  17.8 3.1 %collective-permute-start.12 = (s32[128]{0:T(128)}, s32[128]{0:T(128)S(1)}, u32[]{:S(2)}, u32[]{:S(2)}) collective-permute-start(s32[128]{0:T(128)} %param.19), channel_id=1, source_target_pairs={{0,6},{1,7},{2,0},{3,1},{4,2},{5,3},{6,4},{7,5},{8,14},{9,15},{10,... | collective-permute-start | bytes 1544 | tf_op jit(solution)/shard_map/ppermute | solution.py:23
  20.9 3.7 %collective-permute-start.13 = (s32[128]{0:T(128)}, s32[128]{0:T(128)S(1)}, u32[]{:S(2)}, u32[]{:S(2)}) collective-permute-start(s32[128]{0:T(128)} %param.19), channel_id=1, source_target_pairs={{0,4},{1,5},{2,6},{3,7},{4,0},{5,1},{6,2},{7,3},{8,12},{9,13},{10,... | collective-permute-start | bytes 1544 | tf_op jit(solution)/shard_map/ppermute | solution.py:23
  24.6 3.1 %collective-permute-start.14 = (s32[128]{0:T(128)}, s32[128]{0:T(128)S(1)}, u32[]{:S(2)}, u32[]{:S(2)}) collective-permute-start(s32[128]{0:T(128)} %param.19), channel_id=1, source_target_pairs={{0,2},{1,3},{2,4},{3,5},{4,6},{5,7},{6,0},{7,1},{8,10},{9,11},{10,... | collective-permute-start | bytes 1544 | tf_op jit(solution)/shard_map/ppermute | solution.py:23
  34.4 2.4 collective-permute-start.2
  36.8 14.8 %collective-permute-start.3 = (bf16[48,1536]{1,0:T(8,128)(2,1)S(1)}, bf16[48,1536]{1,0:T(8,128)(2,1)S(1)}, u32[]{:S(2)}, u32[]{:S(2)}) collective-permute-start(bf16[48,1536]{1,0:T(8,128)(2,1)S(1)} %fusion.56), channel_id=1, source_target_pairs={{0,8},{1,9},{2,10},{3,11},{4,12},{5,13},{6,14},{7,15},{8,0},{9,1},... | collective-permute-start | bytes 442376 | tf_op jit(solution)/shard_map/ppermute | solution.py:23
  51.6 1.9 collective-permute-start.15
  54.7 1.9 collective-permute-start.16
  56.7 13.9 %collective-permute-done.3 = bf16[48,1536]{1,0:T(8,128)(2,1)S(1)} collective-permute-done((bf16[48,1536]{1,0:T(8,128)(2,1)S(1)}, bf16[48,1536]{1,0:T(8,128)(2,1)S(1)}, u32[]{:S(2)}, u32[]{:S(2)}) %collective-permute-start.3) | collective-permute-done | bytes 147488 | tf_op jit(solution)/shard_map/ppermute | solution.py:23
  70.6 2.3 collective-permute-start.4
  73.6 4.0 %collective-permute-done.4 = bf16[48,1536]{1,0:T(8,128)(2,1)S(1)} collective-permute-done((bf16[48,1536]{1,0:T(8,128)(2,1)S(1)}, bf16[48,1536]{1,0:T(8,128)(2,1)S(1)}, u32[]{:S(2)}, u32[]{:S(2)}) %collective-permute-start.4) | collective-permute-done | bytes 147488 | tf_op jit(solution)/shard_map/ppermute | solution.py:23
  77.6 5.4 %collective-permute-start.5 = (bf16[48,1536]{1,0:T(8,128)(2,1)S(1)}, bf16[48,1536]{1,0:T(8,128)(2,1)S(1)}, u32[]{:S(2)}, u32[]{:S(2)}) collective-permute-start(bf16[48,1536]{1,0:T(8,128)(2,1)S(1)} %collective-permute-done.3), channel_id=1, source_target_pairs={{0,256},{1,257},{2,258},{3,259},{4,260},{5,261},{6,262},{7,263},{8... | collective-permute-start | bytes 442376 | tf_op jit(solution)/shard_map/ppermute | solution.py:23
  83.7 1.9 collective-permute-done.16
  85.6 3.5 %collective-permute-start.6 = (bf16[48,1536]{1,0:T(8,128)(2,1)S(1)}, bf16[48,1536]{1,0:T(8,128)(2,1)S(1)}, u32[]{:S(2)}, u32[]{:S(2)}) collective-permute-start(bf16[48,1536]{1,0:T(8,128)(2,1)S(1)} %collective-permute-done.3), channel_id=1, source_target_pairs={{0,128},{1,129},{2,130},{3,131},{4,132},{5,133},{6,134},{7,135},{8... | collective-permute-start | bytes 442376 | tf_op jit(solution)/shard_map/ppermute | solution.py:23
  89.1 1.9 collective-permute-start.17
  91.7 5.7 %collective-permute-done.17 = bf16[192,512]{1,0:T(8,128)(2,1)S(1)} collective-permute-done((bf16[192,512]{1,0:T(8,128)(2,1)S(1)}, bf16[192,512]{1,0:T(8,128)(2,1)S(1)}, u32[]{:S(2)}, u32[]{:S(2)}) %collective-permute-start.17) | collective-permute-done | bytes 196640 | tf_op jit(solution)/shard_map/ppermute | solution.py:23
  97.4 1.9 collective-permute-start.7
  100.3 9.6 %collective-permute-start.18 = (bf16[32,1536]{1,0:T(8,128)(2,1)}, bf16[32,1536]{1,0:T(8,128)(2,1)}, u32[]{:S(2)}, u32[]{:S(2)}) collective-permute-start(bf16[32,1536]{1,0:T(8,128)(2,1)} %constant_dynamic-slice_fusion), channel_id=1, source_target_pairs={{0,8},{1,9},{2,10},{3,11},{4,12},{5,13},{6,14},{7,15},{8,0},{9,1},... | collective-permute-start | bytes 294920 | tf_op jit(solution)/shard_map/ppermute | solution.py:23
  116.0 2.1 collective-permute-start.8
  120.2 1.6 convolution_convert_fusion.2
  122.5 2.2 collective-permute-start.9
  130.0 5.0 %collective-permute-start.10 = (bf16[1024,128]{0,1:T(8,128)(2,1)S(1)}, bf16[1024,128]{0,1:T(8,128)(2,1)S(1)}, u32[]{:S(2)}, u32[]{:S(2)}) collective-permute-start(bf16[1024,128]{0,1:T(8,128)(2,1)S(1)} %get-tuple-element.13), channel_id=1, source_target_pairs={{0,8},{1,9},{2,10},{3,11},{4,12},{5,13},{6,14},{7,15},{8,0},{9,1},... | collective-permute-start | bytes 786440 | tf_op jit(solution)/shard_map/ppermute | solution.py:23
  135.0 1.6 compare_and_fusion
  136.6 25.3 %collective-permute-done.10 = bf16[1024,128]{0,1:T(8,128)(2,1)S(1)} collective-permute-done((bf16[1024,128]{0,1:T(8,128)(2,1)S(1)}, bf16[1024,128]{0,1:T(8,128)(2,1)S(1)}, u32[]{:S(2)}, u32[]{:S(2)}) %collective-permute-start.10) | collective-permute-done | bytes 262176 | tf_op jit(solution)/shard_map/ppermute | solution.py:23
  161.9 2.1 collective-permute-start.11
  164.0 1.8 fusion.8
  166.8 5.3 %collective-permute-done.11 = bf16[1024,128]{0,1:T(8,128)(2,1)} collective-permute-done((bf16[1024,128]{0,1:T(8,128)(2,1)S(1)}, bf16[1024,128]{0,1:T(8,128)(2,1)}, u32[]{:S(2)}, u32[]{:S(2)}) %collective-permute-start.11) | collective-permute-done | bytes 262176 | tf_op jit(solution)/shard_map/ppermute | solution.py:23
  173.8 3.3 %fusion.126 = f32[2,512]{1,0:T(2,128)S(1)} fusion(pred[512,1536]{1,0:T(8,128)(4,1)S(1)} %copy-done.6, bf16[1024,64]{0,1:T(8,128)(2,1)S(1)} %get-tuple-element.11, bf16[1024,64]{0,1:T(8,128)(2,1)} %copy-done.10, bf16[1,1024,64]{1,2,0:T(8,128)(2,1)} %get-tuple-element.6, bf16[1,1024,64]{1,2,0:T(8,128)(2,1)} %get-tuple-element.7), kind=kOutput, calls=%fused_computation.196 | convolution fusion | flops 208078336 | bytes 1314816 | tf_op jit(solution)/shard_map/sub | solution.py:87
  177.1 4.7 %fusion.23 = bf16[64,2,512]{2,0,1:T(8,128)(2,1)} fusion(f32[2,512]{1,0:T(2,128)S(1)} %fusion.126, pred[512,1536]{1,0:T(8,128)(4,1)S(1)} %copy-done.6, bf16[1024,64]{0,1:T(8,128)(2,1)} %get-tuple-element.10, bf16[1024,64]{0,1:T(8,128)(2,1)} %copy-done.12, bf16[1024,64]{0,1:T(8,128)(2,1)} %copy-done.15, bf16[1024,64]{0,1:T(8,128)(2,1)} %copy-done.10, ...), kind=kOutput, calls=%fused_computation.42 | convolution fusion | flops 411437568 | bytes 1708032 | tf_op jit(solution)/shard_map/hqk,kd->qhd/dot_general | solution.py:89
  181.8 3.4 %fusion.123 = f32[2,512]{1,0:T(2,128)S(1)} fusion(pred[512,1536]{1,0:T(8,128)(4,1)S(1)} %copy-done.5, bf16[1024,64]{0,1:T(8,128)(2,1)} %copy-done.10, bf16[1024,64]{0,1:T(8,128)(2,1)} %copy-done.15, bf16[1,1024,64]{1,2,0:T(8,128)(2,1)} %get-tuple-element.7, bf16[1,1024,64]{1,2,0:T(8,128)(2,1)} %get-tuple-element.6), kind=kOutput, calls=%fused_computation.195 | convolution fusion | flops 208274944 | bytes 1314816 | tf_op jit(solution)/shard_map/sub | solution.py:87
  185.2 3.8 %fusion.22 = bf16[64,2,512]{2,0,1:T(8,128)(2,1)S(1)} fusion(f32[2,512]{1,0:T(2,128)S(1)} %fusion.123, pred[512,1536]{1,0:T(8,128)(4,1)S(1)} %copy-done.5, bf16[1024,64]{0,1:T(8,128)(2,1)S(1)} %copy-done.13, bf16[1024,64]{0,1:T(8,128)(2,1)S(1)} %copy-done.14, bf16[1024,64]{0,1:T(8,128)(2,1)S(1)} %copy-done.11, bf16[1024,64]{0,1:T(8,128)(2,1)S(1)} %copy-done.16, ...), kind=kOutput, calls=%fused_computation.41 | convolution fusion | flops 411634176 | bytes 1708032 | tf_op jit(solution)/shard_map/hqk,kd->qhd/dot_general | solution.py:89
  190.0 4.4 %all-to-all-start = ((bf16[8,256,128]{2,1,0:T(8,128)(2,1)}), bf16[8,256,128]{2,1,0:T(8,128)(2,1)S(1)}, u32[]{:S(2)}, u32[]{:S(2)}) async-start(bf16[8,256,128]{2,1,0:T(8,128)(2,1)} %pad_maximum_fusion.1), calls=%async_computation | async-start | bytes 1048576 | tf_op jit(solution)/shard_map/all_to_all | solution.py:160
  194.9 2.1 collective-permute-start.19
  197.0 7.8 %all-to-all-done = bf16[8,256,128]{2,1,0:T(8,128)(2,1)S(1)} async-done(((bf16[8,256,128]{2,1,0:T(8,128)(2,1)}), bf16[8,256,128]{2,1,0:T(8,128)(2,1)S(1)}, u32[]{:S(2)}, u32[]{:S(2)}) %all-to-all-start) | async-done | bytes 524320 | tf_op jit(solution)/shard_map/all_to_all | solution.py:160
  205.1 2.8 broadcast_select_fusion
  207.9 1.9 collective-permute-start.20
  209.8 2.6 multiply_reduce_fusion
  212.4 1.6 convolution_convert_fusion
  214.0 4.3 %all-to-all-start.1 = ((bf16[8,48,1536]{2,1,0:T(8,128)(2,1)}), bf16[8,48,1536]{2,1,0:T(8,128)(2,1)}, u32[]{:S(2)}, u32[]{:S(2)}) async-start(bf16[8,48,1536]{2,1,0:T(8,128)(2,1)} %bitcast.44), calls=%async_computation.1 | async-start | bytes 2359296 | tf_op jit(solution)/shard_map/all_to_all | solution.py:202
  219.4 16.0 %all_gather.11 = bf16[256,1536]{1,0:T(8,128)(2,1)S(1)} all-gather(bf16[64,1536]{1,0:T(8,128)(2,1)S(1)} %maximum_select_fusion.3), channel_id=1, replica_groups=mesh['y'=4,'zl'=8,'zh'=2,'x'=4,'c'=2] {'y'}, dimensions={0}, use_global_device_ids=true | all-gather | bytes 983040 | tf_op jit(solution)/shard_map/all_gather | solution.py:181
  236.4 1.9 collective-permute-start.21
  238.4 2.6 fusion.131
  241.0 2.2 fusion.19
  243.7 2.7 fusion.13
  246.4 4.9 %all-to-all-start.2 = ((bf16[8,48,1536]{2,1,0:T(8,128)(2,1)}), bf16[8,48,1536]{2,1,0:T(8,128)(2,1)S(1)}, u32[]{:S(2)}, u32[]{:S(2)}) async-start(bf16[8,48,1536]{2,1,0:T(8,128)(2,1)} %bitcast.46), calls=%async_computation.2 | async-start | bytes 2359296 | tf_op jit(solution)/shard_map/all_to_all | solution.py:213
  253.3 15.4 %all-to-all-done.2 = bf16[8,48,1536]{2,1,0:T(8,128)(2,1)S(1)} async-done(((bf16[8,48,1536]{2,1,0:T(8,128)(2,1)}), bf16[8,48,1536]{2,1,0:T(8,128)(2,1)S(1)}, u32[]{:S(2)}, u32[]{:S(2)}) %all-to-all-start.2) | async-done | bytes 1179680 | tf_op jit(solution)/shard_map/all_to_all | solution.py:213
  (152 shorter events, 36.2 us)
Async XLA Ops:
  7.2 21.8 %copy-start.19 = (s32[128,2]{0,1:T(2,128)S(1)}, s32[128,2]{0,1:T(2,128)}, u32[]{:S(2)}) copy-start(s32[128,2]{0,1:T(2,128)} %param.20) | copy-start | bytes 3076
  7.2 22.2 %copy-start.22 = (s32[1,128]{1,0:T(1,128)S(1)}, s32[1,128]{1,0:T(1,128)}, u32[]{:S(2)}) copy-start(s32[1,128]{1,0:T(1,128)} %param.25) | copy-start | bytes 1540
  7.2 23.3 %copy-start.4 = (bf16[1536,256]{1,0:T(8,128)(2,1)S(1)}, bf16[1536,256]{1,0:T(8,128)(2,1)}, u32[]{:S(2)}) copy-start(bf16[1536,256]{1,0:T(8,128)(2,1)} %param.22) | copy-start | bytes 2359300
  7.2 197.9 %all-gather.5.cloned.1.call-start = ((), (), s32[]{:S(2)}) async-start(), calls=%async_computation.4 | async-start | bytes 1966080 | tf_op jit(solution)/shard_map/all_gather | solution.py:181
  8.5 22.1 %copy-start.8 = (bf16[1536,64]{0,1:T(8,128)(2,1)S(1)}, bf16[1536,64]{0,1:T(8,128)(2,1)}, u32[]{:S(2)}) copy-start(bf16[1536,64]{0,1:T(8,128)(2,1)} %param.16) | copy-start | bytes 589828
  8.5 22.1 %copy-start.9 = (bf16[1536,64]{0,1:T(8,128)(2,1)S(1)}, bf16[1536,64]{0,1:T(8,128)(2,1)}, u32[]{:S(2)}) copy-start(bf16[1536,64]{0,1:T(8,128)(2,1)} %param.17) | copy-start | bytes 589828
  10.4 105.5 %collective-permute-start = (bf16[128,1536]{1,0:T(8,128)(2,1)}, bf16[128,1536]{1,0:T(8,128)(2,1)}, u32[]{:S(2)}, u32[]{:S(2)}) collective-permute-start(bf16[128,1536]{1,0:T(8,128)(2,1)} %fusion.30), channel_id=1, source_target_pairs={{0,6},{1,7},{2,0},{3,1},{4,2},{5,3},{6,4},{7,5},{8,14},{9,15},{10,... | collective-permute-start | bytes 1179656 | tf_op jit(solution)/shard_map/ppermute | solution.py:23
  15.1 103.0 %collective-permute-start.1 = (bf16[128,1536]{1,0:T(8,128)(2,1)}, bf16[128,1536]{1,0:T(8,128)(2,1)}, u32[]{:S(2)}, u32[]{:S(2)}) collective-permute-start(bf16[128,1536]{1,0:T(8,128)(2,1)} %fusion.30), channel_id=1, source_target_pairs={{0,4},{1,5},{2,6},{3,7},{4,0},{5,1},{6,2},{7,3},{8,12},{9,13},{10,... | collective-permute-start | bytes 1179656 | tf_op jit(solution)/shard_map/ppermute | solution.py:23
  17.8 16.5 %collective-permute-start.12 = (s32[128]{0:T(128)}, s32[128]{0:T(128)S(1)}, u32[]{:S(2)}, u32[]{:S(2)}) collective-permute-start(s32[128]{0:T(128)} %param.19), channel_id=1, source_target_pairs={{0,6},{1,7},{2,0},{3,1},{4,2},{5,3},{6,4},{7,5},{8,14},{9,15},{10,... | collective-permute-start | bytes 1544 | tf_op jit(solution)/shard_map/ppermute | solution.py:23
  20.9 15.9 %collective-permute-start.13 = (s32[128]{0:T(128)}, s32[128]{0:T(128)S(1)}, u32[]{:S(2)}, u32[]{:S(2)}) collective-permute-start(s32[128]{0:T(128)} %param.19), channel_id=1, source_target_pairs={{0,4},{1,5},{2,6},{3,7},{4,0},{5,1},{6,2},{7,3},{8,12},{9,13},{10,... | collective-permute-start | bytes 1544 | tf_op jit(solution)/shard_map/ppermute | solution.py:23
  24.6 27.0 %collective-permute-start.14 = (s32[128]{0:T(128)}, s32[128]{0:T(128)S(1)}, u32[]{:S(2)}, u32[]{:S(2)}) collective-permute-start(s32[128]{0:T(128)} %param.19), channel_id=1, source_target_pairs={{0,2},{1,3},{2,4},{3,5},{4,6},{5,7},{6,0},{7,1},{8,10},{9,11},{10,... | collective-permute-start | bytes 1544 | tf_op jit(solution)/shard_map/ppermute | solution.py:23
  27.7 3.6 %copy-start.7 = (bf16[64,1536]{1,0:T(8,128)(2,1)S(1)}, bf16[64,1536]{1,0:T(8,128)(2,1)}, u32[]{:S(2)}) copy-start(bf16[64,1536]{1,0:T(8,128)(2,1)} %param.18) | copy-start | bytes 589828
  31.4 20.2 %copy-start.21 = (s32[128]{0:T(128)S(1)}, s32[128]{0:T(128)}, u32[]{:S(2)}) copy-start(s32[128]{0:T(128)} %param.19) | copy-start | bytes 1540
  34.4 83.8 %collective-permute-start.2 = (bf16[128,1536]{1,0:T(8,128)(2,1)}, bf16[128,1536]{1,0:T(8,128)(2,1)}, u32[]{:S(2)}, u32[]{:S(2)}) collective-permute-start(bf16[128,1536]{1,0:T(8,128)(2,1)} %fusion.30), channel_id=1, source_target_pairs={{0,2},{1,3},{2,4},{3,5},{4,6},{5,7},{6,0},{7,1},{8,10},{9,11},{10,... | collective-permute-start | bytes 1179656 | tf_op jit(solution)/shard_map/ppermute | solution.py:23
  36.8 33.8 %collective-permute-start.3 = (bf16[48,1536]{1,0:T(8,128)(2,1)S(1)}, bf16[48,1536]{1,0:T(8,128)(2,1)S(1)}, u32[]{:S(2)}, u32[]{:S(2)}) collective-permute-start(bf16[48,1536]{1,0:T(8,128)(2,1)S(1)} %fusion.56), channel_id=1, source_target_pairs={{0,8},{1,9},{2,10},{3,11},{4,12},{5,13},{6,14},{7,15},{8,0},{9,1},... | collective-permute-start | bytes 442376 | tf_op jit(solution)/shard_map/ppermute | solution.py:23
  51.6 3.1 %collective-permute-start.15 = (s32[4,128]{1,0:T(4,128)S(1)}, s32[4,128]{1,0:T(4,128)S(1)}, u32[]{:S(2)}, u32[]{:S(2)}) collective-permute-start(s32[4,128]{1,0:T(4,128)S(1)} %get-tuple-element.17), channel_id=1, source_target_pairs={{0,1},{1,0},{2,3},{3,2},{4,5},{5,4},{6,7},{7,6},{8,9},{9,8},{10,11... | collective-permute-start | bytes 6152 | tf_op jit(solution)/shard_map/ppermute | solution.py:23
  54.7 30.9 %collective-permute-start.16 = (bf16[192,512]{1,0:T(8,128)(2,1)S(1)}, bf16[192,512]{1,0:T(8,128)(2,1)S(1)}, u32[]{:S(2)}, u32[]{:S(2)}) collective-permute-start(bf16[192,512]{1,0:T(8,128)(2,1)S(1)} %constant_dynamic-slice_fusion.1), channel_id=1, source_target_pairs={{0,8},{1,9},{2,10},{3,11},{4,12},{5,13},{6,14},{7,15},{8,0},{9,1},... | collective-permute-start | bytes 589832 | tf_op jit(solution)/shard_map/ppermute | solution.py:23
  70.6 7.0 %collective-permute-start.4 = (bf16[48,1536]{1,0:T(8,128)(2,1)S(1)}, bf16[48,1536]{1,0:T(8,128)(2,1)S(1)}, u32[]{:S(2)}, u32[]{:S(2)}) collective-permute-start(bf16[48,1536]{1,0:T(8,128)(2,1)S(1)} %collective-permute-done.3), channel_id=1, source_target_pairs={{0,384},{1,385},{2,386},{3,387},{4,388},{5,389},{6,390},{7,391},{8... | collective-permute-start | bytes 442376 | tf_op jit(solution)/shard_map/ppermute | solution.py:23
  77.6 11.4 %collective-permute-start.5 = (bf16[48,1536]{1,0:T(8,128)(2,1)S(1)}, bf16[48,1536]{1,0:T(8,128)(2,1)S(1)}, u32[]{:S(2)}, u32[]{:S(2)}) collective-permute-start(bf16[48,1536]{1,0:T(8,128)(2,1)S(1)} %collective-permute-done.3), channel_id=1, source_target_pairs={{0,256},{1,257},{2,258},{3,259},{4,260},{5,261},{6,262},{7,263},{8... | collective-permute-start | bytes 442376 | tf_op jit(solution)/shard_map/ppermute | solution.py:23
  85.6 14.7 %collective-permute-start.6 = (bf16[48,1536]{1,0:T(8,128)(2,1)S(1)}, bf16[48,1536]{1,0:T(8,128)(2,1)S(1)}, u32[]{:S(2)}, u32[]{:S(2)}) collective-permute-start(bf16[48,1536]{1,0:T(8,128)(2,1)S(1)} %collective-permute-done.3), channel_id=1, source_target_pairs={{0,128},{1,129},{2,130},{3,131},{4,132},{5,133},{6,134},{7,135},{8... | collective-permute-start | bytes 442376 | tf_op jit(solution)/shard_map/ppermute | solution.py:23
  89.1 8.3 %collective-permute-start.17 = (bf16[192,512]{1,0:T(8,128)(2,1)S(1)}, bf16[192,512]{1,0:T(8,128)(2,1)S(1)}, u32[]{:S(2)}, u32[]{:S(2)}) collective-permute-start(bf16[192,512]{1,0:T(8,128)(2,1)S(1)} %collective-permute-done.16), channel_id=1, source_target_pairs={{0,16},{1,17},{2,18},{3,19},{4,20},{5,21},{6,22},{7,23},{8,24},{9,... | collective-permute-start | bytes 589832 | tf_op jit(solution)/shard_map/ppermute | solution.py:23
  97.4 22.8 %collective-permute-start.7 = (bf16[128,1536]{1,0:T(8,128)(2,1)}, bf16[128,1536]{1,0:T(8,128)(2,1)}, u32[]{:S(2)}, u32[]{:S(2)}) collective-permute-start(bf16[128,1536]{1,0:T(8,128)(2,1)} %pad_maximum_fusion.2), channel_id=1, source_target_pairs={{0,1},{1,0},{2,3},{3,2},{4,5},{5,4},{6,7},{7,6},{8,9},{9,8},{10,11... | collective-permute-start | bytes 1179656 | tf_op jit(solution)/shard_map/ppermute | solution.py:23
  100.2 109.6 %all-gather.3.cloned.1.call-start = ((), (), s32[]{:S(2)}) async-start(), calls=%async_computation.3 | async-start | bytes 3538944 | tf_op jit(solution)/shard_map/all_gather | solution.py:165
  100.3 94.6 %collective-permute-start.18 = (bf16[32,1536]{1,0:T(8,128)(2,1)}, bf16[32,1536]{1,0:T(8,128)(2,1)}, u32[]{:S(2)}, u32[]{:S(2)}) collective-permute-start(bf16[32,1536]{1,0:T(8,128)(2,1)} %constant_dynamic-slice_fusion), channel_id=1, source_target_pairs={{0,8},{1,9},{2,10},{3,11},{4,12},{5,13},{6,14},{7,15},{8,0},{9,1},... | collective-permute-start | bytes 294920 | tf_op jit(solution)/shard_map/ppermute | solution.py:23
  116.0 5.9 %collective-permute-start.8 = (bf16[128,1536]{1,0:T(8,128)(2,1)}, bf16[128,1536]{1,0:T(8,128)(2,1)S(1)}, u32[]{:S(2)}, u32[]{:S(2)}) collective-permute-start(bf16[128,1536]{1,0:T(8,128)(2,1)} %slice.124), channel_id=1, source_target_pairs={{0,1},{1,0},{2,3},{3,2},{4,5},{5,4},{6,7},{7,6},{8,9},{9,8},{10,11... | collective-permute-start | bytes 1179656 | tf_op jit(solution)/shard_map/ppermute | solution.py:23
  122.5 3.4 %collective-permute-start.9 = (bf16[512,256]{0,1:T(8,128)(2,1)S(1)}, bf16[512,256]{0,1:T(8,128)(2,1)S(1)}, u32[]{:S(2)}, u32[]{:S(2)}) collective-permute-start(bf16[512,256]{0,1:T(8,128)(2,1)S(1)} %pad_maximum_fusion.5), channel_id=1, source_target_pairs={{0,1},{1,0},{2,3},{3,2},{4,5},{5,4},{6,7},{7,6},{8,9},{9,8},{10,11... | collective-permute-start | bytes 786440 | tf_op jit(solution)/shard_map/ppermute | solution.py:23
  130.0 31.8 %collective-permute-start.10 = (bf16[1024,128]{0,1:T(8,128)(2,1)S(1)}, bf16[1024,128]{0,1:T(8,128)(2,1)S(1)}, u32[]{:S(2)}, u32[]{:S(2)}) collective-permute-start(bf16[1024,128]{0,1:T(8,128)(2,1)S(1)} %get-tuple-element.13), channel_id=1, source_target_pairs={{0,8},{1,9},{2,10},{3,11},{4,12},{5,13},{6,14},{7,15},{8,0},{9,1},... | collective-permute-start | bytes 786440 | tf_op jit(solution)/shard_map/ppermute | solution.py:23
  161.9 10.3 %collective-permute-start.11 = (bf16[1024,128]{0,1:T(8,128)(2,1)S(1)}, bf16[1024,128]{0,1:T(8,128)(2,1)}, u32[]{:S(2)}, u32[]{:S(2)}) collective-permute-start(bf16[1024,128]{0,1:T(8,128)(2,1)S(1)} %collective-permute-done.10), channel_id=1, source_target_pairs={{0,16},{1,17},{2,18},{3,19},{4,20},{5,21},{6,22},{7,23},{16,32},{1... | collective-permute-start | bytes 786440 | tf_op jit(solution)/shard_map/ppermute | solution.py:23
  166.1 7.6 %copy-start.6 = (pred[512,1536]{1,0:T(8,128)(4,1)S(1)}, pred[512,1536]{1,0:T(8,128)(4,1)}, u32[]{:S(2)}) copy-start(pred[512,1536]{1,0:T(8,128)(4,1)} %fusion.8) | copy-start | bytes 2359300
  173.8 3.3 %copy-start.15 = (bf16[1024,64]{0,1:T(8,128)(2,1)}, bf16[1024,64]{0,1:T(8,128)(2,1)S(1)}, u32[]{:S(2)}) copy-start(bf16[1024,64]{0,1:T(8,128)(2,1)S(1)} %get-tuple-element.11) | copy-start | bytes 393220
  177.1 4.7 %copy-start.5 = (pred[512,1536]{1,0:T(8,128)(4,1)S(1)}, pred[512,1536]{1,0:T(8,128)(4,1)}, u32[]{:S(2)}) copy-start(pred[512,1536]{1,0:T(8,128)(4,1)} %compare_and_fusion) | copy-start | bytes 2359300
  181.8 3.4 %copy-start.11 = (bf16[1024,64]{0,1:T(8,128)(2,1)S(1)}, bf16[1024,64]{0,1:T(8,128)(2,1)}, u32[]{:S(2)}) copy-start(bf16[1024,64]{0,1:T(8,128)(2,1)} %copy-done.10) | copy-start | bytes 393220
  181.8 3.4 %copy-start.13 = (bf16[1024,64]{0,1:T(8,128)(2,1)S(1)}, bf16[1024,64]{0,1:T(8,128)(2,1)}, u32[]{:S(2)}) copy-start(bf16[1024,64]{0,1:T(8,128)(2,1)} %copy-done.12) | copy-start | bytes 393220
  181.8 3.4 %copy-start.14 = (bf16[1024,64]{0,1:T(8,128)(2,1)S(1)}, bf16[1024,64]{0,1:T(8,128)(2,1)}, u32[]{:S(2)}) copy-start(bf16[1024,64]{0,1:T(8,128)(2,1)} %get-tuple-element.10) | copy-start | bytes 393220
  181.8 3.4 %copy-start.16 = (bf16[1024,64]{0,1:T(8,128)(2,1)S(1)}, bf16[1024,64]{0,1:T(8,128)(2,1)}, u32[]{:S(2)}) copy-start(bf16[1024,64]{0,1:T(8,128)(2,1)} %copy-done.15) | copy-start | bytes 393220
  185.2 3.8 %copy-start.17 = (bf16[64,2,512]{2,0,1:T(8,128)(2,1)S(1)}, bf16[64,2,512]{2,0,1:T(8,128)(2,1)}, u32[]{:S(2)}) copy-start(bf16[64,2,512]{2,0,1:T(8,128)(2,1)} %fusion.23) | copy-start | bytes 393220
  190.0 14.8 %all-to-all-start = ((bf16[8,256,128]{2,1,0:T(8,128)(2,1)}), bf16[8,256,128]{2,1,0:T(8,128)(2,1)S(1)}, u32[]{:S(2)}, u32[]{:S(2)}) async-start(bf16[8,256,128]{2,1,0:T(8,128)(2,1)} %pad_maximum_fusion.1), calls=%async_computation | async-start | bytes 1048576 | tf_op jit(solution)/shard_map/all_to_all | solution.py:160
  194.9 23.4 %collective-permute-start.19 = (bf16[32,1536]{1,0:T(8,128)(2,1)}, bf16[32,1536]{1,0:T(8,128)(2,1)S(1)}, u32[]{:S(2)}, u32[]{:S(2)}) collective-permute-start(bf16[32,1536]{1,0:T(8,128)(2,1)} %collective-permute-done.18), channel_id=1, source_target_pairs={{0,16},{1,17},{2,18},{3,19},{4,20},{5,21},{6,22},{7,23},{8,24},{9,... | collective-permute-start | bytes 294920 | tf_op jit(solution)/shard_map/ppermute | solution.py:23
  205.1 4.8 %copy-start = (bf16[128,1536]{1,0:T(8,128)(2,1)S(1)}, bf16[128,1536]{1,0:T(8,128)(2,1)}, u32[]{:S(2)}) copy-start(bf16[128,1536]{1,0:T(8,128)(2,1)} %param.13) | copy-start | bytes 1179652
  207.9 30.5 %collective-permute-start.20 = (bf16[1536,512]{1,0:T(8,128)(2,1)}, bf16[1536,512]{1,0:T(8,128)(2,1)}, u32[]{:S(2)}, u32[]{:S(2)}) collective-permute-start(bf16[1536,512]{1,0:T(8,128)(2,1)} %broadcast_select_fusion), channel_id=1, source_target_pairs={{0,1},{1,0},{2,3},{3,2},{4,5},{5,4},{6,7},{7,6},{8,9},{9,8},{10,11... | collective-permute-start | bytes 4718600 | tf_op jit(solution)/shard_map/ppermute | solution.py:23
  209.8 2.6 copy-start.18
  214.0 24.3 %all-to-all-start.1 = ((bf16[8,48,1536]{2,1,0:T(8,128)(2,1)}), bf16[8,48,1536]{2,1,0:T(8,128)(2,1)}, u32[]{:S(2)}, u32[]{:S(2)}) async-start(bf16[8,48,1536]{2,1,0:T(8,128)(2,1)} %bitcast.44), calls=%async_computation.1 | async-start | bytes 2359296 | tf_op jit(solution)/shard_map/all_to_all | solution.py:202
  218.3 17.1 %copy-start.1 = (bf16[256,1536]{1,0:T(8,128)(2,1)S(1)}, bf16[256,1536]{1,0:T(8,128)(2,1)}, u32[]{:S(2)}) copy-start(bf16[256,1536]{1,0:T(8,128)(2,1)} %param.24) | copy-start | bytes 2359300
  236.4 7.3 %collective-permute-start.21 = (bf16[256,1536]{1,0:T(8,128)(2,1)}, bf16[256,1536]{1,0:T(8,128)(2,1)}, u32[]{:S(2)}, u32[]{:S(2)}) collective-permute-start(bf16[256,1536]{1,0:T(8,128)(2,1)} %broadcast_select_fusion.1), channel_id=1, source_target_pairs={{0,1},{1,0},{2,3},{3,2},{4,5},{5,4},{6,7},{7,6},{8,9},{9,8},{10,11... | collective-permute-start | bytes 2359304 | tf_op jit(solution)/shard_map/ppermute | solution.py:23
  238.3 2.7 copy-start.3
  241.0 2.2 copy-start.2
  246.4 4.9 %copy-start.20 = (f32[128,2]{0,1:T(2,128)S(1)}, f32[128,2]{0,1:T(2,128)}, u32[]{:S(2)}) copy-start(f32[128,2]{0,1:T(2,128)} %param.21) | copy-start | bytes 3076
  246.4 22.3 %all-to-all-start.2 = ((bf16[8,48,1536]{2,1,0:T(8,128)(2,1)}), bf16[8,48,1536]{2,1,0:T(8,128)(2,1)S(1)}, u32[]{:S(2)}, u32[]{:S(2)}) async-start(bf16[8,48,1536]{2,1,0:T(8,128)(2,1)} %bitcast.46), calls=%async_computation.2 | async-start | bytes 2359296 | tf_op jit(solution)/shard_map/all_to_all | solution.py:213
  (2 other events, 1.3 us)
Sparse Core Ops, SparseCore 0:
  100.3 32.7 all-gather.4
  135.3 36.5 all-gather.2
where the time goes:
time: 279 us; the launch traced here: 277 us
  starting transfers between devices  94 us (34%)
  waiting for transfers between devices  80.8 us (29%)
  matrix products  32.4 us (12%)
  other arithmetic  21.8 us (8%)
  local copies, waits for them, and re-layouts  17 us (6%)
  blocking collectives  16 us (6%)
  between operations  15.1 us (5%)
    ppermute x22, starting transfers between devices, permute(): return lax.ppermute(block, AXES, route)  80.3 us
    ppermute x22, waiting for transfers between devices, permute(): return lax.ppermute(block, AXES, route)  57.5 us
    all_gather x1, blocking collectives, far_weight(): return lax.all_gather(pair, 'y', axis=0, tiled=True)  16 us
    all_to_all x1, waiting for transfers between devices, body(): lax.all_to_all(expert_out.reshape(8, CAP, width), ROW, split_axis=0, conc...  15.4 us
    dot_general x2, matrix products, attend(): jnp.einsum('hqk,kd->qhd', weights, values, preferred_element_type=jnp.flo...  8.46 us
    all_to_all x1, waiting for transfers between devices, body(): lax.all_to_all(joined, ROW, split_axis=0, concat_axis=0, tiled=True)  7.79 us
    sub x2, matrix products, attend(): exponent = jnp.exp(scores - jnp.max(scores, axis=-1, keepdims=True))  6.67 us
    unnamed x55, local copies, waits for them, and re-layouts  5.58 us
  transfers between devices with their start and end apart: 27, of which 10 were waited for; matrix products, arithmetic and copies ran while one was open for 23% of the time, Pallas kernels for 0%

commit v1 on v0

--- a/solution.py
+++ b/solution.py
@@ -178,7 +178,9 @@
             jnp.concatenate([eighth, beside], axis=0),
             jnp.concatenate([beside, eighth], axis=0),
         )
-        return lax.all_gather(pair, "y", axis=0, tiled=True)
+        return jnp.concatenate(
+            lax.all_to_all(jnp.stack([pair] * lax.axis_size("y")), "y", 0, 0), axis=0
+        )
 
     def whole(own):
         far = far_weight(own)

time: 279 us -> 307 us (1.10)
  the two profiles are of different devices: /device:TPU:40 before, /device:TPU:1 now
where the time goes in v1:
time: 307 us; the launch traced here: 305 us
  starting transfers between devices  129 us (42%)
  waiting for transfers between devices  81.9 us (27%)
  matrix products  31.5 us (10%)
  other arithmetic  30.6 us (10%)
  local copies, waits for them, and re-layouts  16.5 us (5%)
  between operations  15 us (5%)
    ppermute x22, starting transfers between devices, permute(): return lax.ppermute(block, AXES, route)  103 us
    ppermute x22, waiting for transfers between devices, permute(): return lax.ppermute(block, AXES, route)  48.7 us
    all_to_all x1, waiting for transfers between devices, body(): lax.all_to_all(expert_out.reshape(8, CAP, width), ROW, split_axis=0, conc...  14.6 us
    all_to_all x2, waiting for transfers between devices, far_weight(): lax.all_to_all(jnp.stack([pair] * lax.axis_size('y')), 'y', 0, 0)  12.4 us
    all_to_all x2, starting transfers between devices, far_weight(): lax.all_to_all(jnp.stack([pair] * lax.axis_size('y')), 'y', 0, 0)  11.8 us
    dot_general x2, matrix products, attend(): jnp.einsum('hqk,kd->qhd', weights, values, preferred_element_type=jnp.flo...  7.79 us
    all_to_all x1, starting transfers between devices, body(): lax.all_to_all(send.reshape(8, CAP, width), ROW, split_axis=0, concat_axi...  6.37 us
    all_to_all x1, waiting for transfers between devices, body(): lax.all_to_all(send.reshape(8, CAP, width), ROW, split_axis=0, concat_axi...  6.31 us
  transfers between devices with their start and end apart: 28, of which 11 were waited for; matrix products, arithmetic and copies ran while one was open for 23% of the time, Pallas kernels for 0%

profile of v1, /device:TPU:1, one launch (start us, length us, event | category | flops | bytes accessed | tf_op | source)
XLA Modules:
  0.0 305.0 jit_solution(3284917312257722220)
XLA Ops:
  8.5 1.9 fusion.27
  10.4 5.2 %collective-permute-start = (bf16[128,1536]{1,0:T(8,128)(2,1)}, bf16[128,1536]{1,0:T(8,128)(2,1)}, u32[]{:S(2)}, u32[]{:S(2)}) collective-permute-start(bf16[128,1536]{1,0:T(8,128)(2,1)} %fusion.27), channel_id=1, source_target_pairs={{0,6},{1,7},{2,0},{3,1},{4,2},{5,3},{6,4},{7,5},{8,14},{9,15},{10,... | collective-permute-start | bytes 1179656 | tf_op jit(solution)/shard_map/ppermute | solution.py:23
  15.6 2.4 collective-permute-start.1
  18.0 2.5 collective-permute-start.12
  20.6 3.8 %collective-permute-start.13 = (s32[128]{0:T(128)}, s32[128]{0:T(128)}, u32[]{:S(2)}, u32[]{:S(2)}) collective-permute-start(s32[128]{0:T(128)} %param.19), channel_id=1, source_target_pairs={{0,4},{1,5},{2,6},{3,7},{4,0},{5,1},{6,2},{7,3},{8,12},{9,13},{10,... | collective-permute-start | bytes 1544 | tf_op jit(solution)/shard_map/ppermute | solution.py:23
  24.3 2.8 collective-permute-start.14
  38.4 1.9 collective-permute-start.2
  40.3 15.6 %collective-permute-start.3 = (bf16[48,1536]{1,0:T(8,128)(2,1)}, bf16[48,1536]{1,0:T(8,128)(2,1)S(1)}, u32[]{:S(2)}, u32[]{:S(2)}) collective-permute-start(bf16[48,1536]{1,0:T(8,128)(2,1)} %fusion.51), channel_id=1, source_target_pairs={{0,8},{1,9},{2,10},{3,11},{4,12},{5,13},{6,14},{7,15},{8,0},{9,1},... | collective-permute-start | bytes 442376 | tf_op jit(solution)/shard_map/ppermute | solution.py:23
  56.6 4.5 %collective-permute-start.15 = (s32[4,128]{1,0:T(4,128)S(1)}, s32[4,128]{1,0:T(4,128)S(1)}, u32[]{:S(2)}, u32[]{:S(2)}) collective-permute-start(s32[4,128]{1,0:T(4,128)S(1)} %get-tuple-element.19), channel_id=1, source_target_pairs={{0,1},{1,0},{2,3},{3,2},{4,5},{5,4},{6,7},{7,6},{8,9},{9,8},{10,11... | collective-permute-start | bytes 6152 | tf_op jit(solution)/shard_map/ppermute | solution.py:23
  64.0 1.9 collective-permute-start.7
  66.0 2.3 compare_and_fusion
  68.3 4.6 %collective-permute-start.4 = (bf16[48,1536]{1,0:T(8,128)(2,1)S(1)}, bf16[48,1536]{1,0:T(8,128)(2,1)S(1)}, u32[]{:S(2)}, u32[]{:S(2)}) collective-permute-start(bf16[48,1536]{1,0:T(8,128)(2,1)S(1)} %collective-permute-done.3), channel_id=1, source_target_pairs={{0,384},{1,385},{2,386},{3,387},{4,388},{5,389},{6,390},{7,391},{8... | collective-permute-start | bytes 442376 | tf_op jit(solution)/shard_map/ppermute | solution.py:23
  72.9 2.7 collective-permute-done.4
  75.6 4.3 %collective-permute-start.5 = (bf16[48,1536]{1,0:T(8,128)(2,1)S(1)}, bf16[48,1536]{1,0:T(8,128)(2,1)S(1)}, u32[]{:S(2)}, u32[]{:S(2)}) collective-permute-start(bf16[48,1536]{1,0:T(8,128)(2,1)S(1)} %collective-permute-done.3), channel_id=1, source_target_pairs={{0,256},{1,257},{2,258},{3,259},{4,260},{5,261},{6,262},{7,263},{8... | collective-permute-start | bytes 442376 | tf_op jit(solution)/shard_map/ppermute | solution.py:23
  79.9 3.1 %collective-permute-done.5 = bf16[48,1536]{1,0:T(8,128)(2,1)S(1)} collective-permute-done((bf16[48,1536]{1,0:T(8,128)(2,1)S(1)}, bf16[48,1536]{1,0:T(8,128)(2,1)S(1)}, u32[]{:S(2)}, u32[]{:S(2)}) %collective-permute-start.5) | collective-permute-done | bytes 147488 | tf_op jit(solution)/shard_map/ppermute | solution.py:23
  83.0 2.9 collective-permute-start.6
  85.9 4.9 %collective-permute-done.6 = bf16[48,1536]{1,0:T(8,128)(2,1)S(1)} collective-permute-done((bf16[48,1536]{1,0:T(8,128)(2,1)S(1)}, bf16[48,1536]{1,0:T(8,128)(2,1)S(1)}, u32[]{:S(2)}, u32[]{:S(2)}) %collective-permute-start.6) | collective-permute-done | bytes 147488 | tf_op jit(solution)/shard_map/ppermute | solution.py:23
  90.8 2.5 collective-permute-start.18
  94.3 10.9 %collective-permute-done.18 = bf16[32,1536]{1,0:T(8,128)(2,1)} collective-permute-done((bf16[32,1536]{1,0:T(8,128)(2,1)}, bf16[32,1536]{1,0:T(8,128)(2,1)}, u32[]{:S(2)}, u32[]{:S(2)}) %collective-permute-start.18) | collective-permute-done | bytes 98336 | tf_op jit(solution)/shard_map/ppermute | solution.py:23
  105.3 2.4 collective-permute-start.16
  107.7 6.1 %collective-permute-start.19 = (bf16[32,1536]{1,0:T(8,128)(2,1)}, bf16[32,1536]{1,0:T(8,128)(2,1)}, u32[]{:S(2)}, u32[]{:S(2)}) collective-permute-start(bf16[32,1536]{1,0:T(8,128)(2,1)} %collective-permute-done.18), channel_id=1, source_target_pairs={{0,16},{1,17},{2,18},{3,19},{4,20},{5,21},{6,22},{7,23},{8,24},{9,... | collective-permute-start | bytes 294920 | tf_op jit(solution)/shard_map/ppermute | solution.py:23
  113.8 16.7 %collective-permute-start.8 = (bf16[128,1536]{1,0:T(8,128)(2,1)S(1)}, bf16[128,1536]{1,0:T(8,128)(2,1)S(1)}, u32[]{:S(2)}, u32[]{:S(2)}) collective-permute-start(bf16[128,1536]{1,0:T(8,128)(2,1)S(1)} %slice.124), channel_id=1, source_target_pairs={{0,1},{1,0},{2,3},{3,2},{4,5},{5,4},{6,7},{7,6},{8,9},{9,8},{10,11... | collective-permute-start | bytes 1179656 | tf_op jit(solution)/shard_map/ppermute | solution.py:23
  134.9 1.9 collective-permute-start.9
  141.8 2.0 collective-permute-start.10
  143.8 1.8 fusion.8
  145.6 20.8 %collective-permute-done.10 = bf16[1024,128]{0,1:T(8,128)(2,1)S(1)} collective-permute-done((bf16[1024,128]{0,1:T(8,128)(2,1)S(1)}, bf16[1024,128]{0,1:T(8,128)(2,1)S(1)}, u32[]{:S(2)}, u32[]{:S(2)}) %collective-permute-start.10) | collective-permute-done | bytes 262176 | tf_op jit(solution)/shard_map/ppermute | solution.py:23
  166.5 11.9 %collective-permute-start.11 = (bf16[1024,128]{0,1:T(8,128)(2,1)S(1)}, bf16[1024,128]{0,1:T(8,128)(2,1)S(1)}, u32[]{:S(2)}, u32[]{:S(2)}) collective-permute-start(bf16[1024,128]{0,1:T(8,128)(2,1)S(1)} %collective-permute-done.10), channel_id=1, source_target_pairs={{0,16},{1,17},{2,18},{3,19},{4,20},{5,21},{6,22},{7,23},{16,32},{1... | collective-permute-start | bytes 786440 | tf_op jit(solution)/shard_map/ppermute | solution.py:23
  180.5 3.7 %all-to-all-start.3 = ((bf16[4,64,1536]{2,1,0:T(8,128)(2,1)}), bf16[4,64,1536]{2,1,0:T(8,128)(2,1)S(1)}, u32[]{:S(2)}, u32[]{:S(2)}) async-start(bf16[4,64,1536]{2,1,0:T(8,128)(2,1)} %stack.138), calls=%async_computation.3 | async-start | bytes 1572864 | tf_op jit(solution)/shard_map/all_to_all | solution.py:182
  185.4 3.6 %fusion.118 = f32[2,512]{1,0:T(2,128)S(1)} fusion(pred[512,1536]{1,0:T(8,128)(4,1)} %compare_and_fusion, bf16[1024,64]{0,1:T(8,128)(2,1)S(1)} %get-tuple-element.10, bf16[1024,64]{0,1:T(8,128)(2,1)S(1)} %get-tuple-element.13, bf16[1,1024,64]{1,2,0:T(8,128)(2,1)} %get-tuple-element.9, bf16[1,1024,64]{1,2,0:T(8,128)(2,1)S(1)} %get-tuple-element.8), kind=kOutput, calls=%fused_computation.192 | convolution fusion | flops 208274944 | bytes 1314816 | tf_op jit(solution)/shard_map/sub | solution.py:87
  189.0 2.4 fusion.121
  191.4 3.8 %fusion.20 = bf16[64,2,512]{2,0,1:T(8,128)(2,1)S(1)} fusion(f32[2,512]{1,0:T(2,128)S(1)} %fusion.121, pred[512,1536]{1,0:T(8,128)(4,1)S(1)} %copy-done.13, bf16[1024,64]{0,1:T(8,128)(2,1)S(1)} %get-tuple-element.12, bf16[1024,64]{0,1:T(8,128)(2,1)S(1)} %get-tuple-element.11, bf16[1024,64]{0,1:T(8,128)(2,1)S(1)} %get-tuple-element.13, ...), kind=kOutput, calls=%fused_computation.40 | convolution fusion | flops 411437568 | bytes 1708032 | tf_op jit(solution)/shard_map/hqk,kd->qhd/dot_general | solution.py:89
  195.2 4.0 %fusion.19 = bf16[64,2,512]{2,0,1:T(8,128)(2,1)S(1)} fusion(f32[2,512]{1,0:T(2,128)S(1)} %fusion.118, pred[512,1536]{1,0:T(8,128)(4,1)} %compare_and_fusion, bf16[1024,64]{0,1:T(8,128)(2,1)S(1)} %get-tuple-element.11, bf16[1024,64]{0,1:T(8,128)(2,1)S(1)} %get-tuple-element.12, bf16[1024,64]{0,1:T(8,128)(2,1)S(1)} %get-tuple-element.10, ...), kind=kOutput, calls=%fused_computation.39 | convolution fusion | flops 411634176 | bytes 1708032 | tf_op jit(solution)/shard_map/hqk,kd->qhd/dot_general | solution.py:89
  201.1 3.9 %all-to-all-start = ((bf16[8,256,128]{2,1,0:T(8,128)(2,1)}), bf16[8,256,128]{2,1,0:T(8,128)(2,1)S(1)}, u32[]{:S(2)}, u32[]{:S(2)}) async-start(bf16[8,256,128]{2,1,0:T(8,128)(2,1)} %pad_maximum_fusion.1), calls=%async_computation | async-start | bytes 1048576 | tf_op jit(solution)/shard_map/all_to_all | solution.py:160
  205.5 2.3 collective-permute-start.17
  208.5 5.5 %collective-permute-done.17 = bf16[192,512]{1,0:T(8,128)(2,1)S(1)} collective-permute-done((bf16[192,512]{1,0:T(8,128)(2,1)}, bf16[192,512]{1,0:T(8,128)(2,1)S(1)}, u32[]{:S(2)}, u32[]{:S(2)}) %collective-permute-start.17) | collective-permute-done | bytes 196640 | tf_op jit(solution)/shard_map/ppermute | solution.py:23
  216.6 8.1 %all-to-all-start.2 = ((bf16[4,384,512]{2,1,0:T(8,128)(2,1)}), bf16[4,384,512]{2,1,0:T(8,128)(2,1)S(1)}, u32[]{:S(2)}, u32[]{:S(2)}) async-start(bf16[4,384,512]{2,1,0:T(8,128)(2,1)} %stack.137), calls=%async_computation.2 | async-start | bytes 3145728 | tf_op jit(solution)/shard_map/all_to_all | solution.py:182
  228.4 2.7 multiply_reduce_fusion
  232.7 11.5 %all-to-all-done.2 = bf16[4,384,512]{2,1,0:T(8,128)(2,1)S(1)} async-done(((bf16[4,384,512]{2,1,0:T(8,128)(2,1)}), bf16[4,384,512]{2,1,0:T(8,128)(2,1)S(1)}, u32[]{:S(2)}, u32[]{:S(2)}) %all-to-all-start.2) | async-done | bytes 1572896 | tf_op jit(solution)/shard_map/all_to_all | solution.py:182
  244.2 6.4 %all-to-all-start.1 = ((bf16[8,48,1536]{2,1,0:T(8,128)(2,1)}), bf16[8,48,1536]{2,1,0:T(8,128)(2,1)}, u32[]{:S(2)}, u32[]{:S(2)}) async-start(bf16[8,48,1536]{2,1,0:T(8,128)(2,1)} %bitcast.44), calls=%async_computation.1 | async-start | bytes 2359296 | tf_op jit(solution)/shard_map/all_to_all | solution.py:204
  250.6 2.9 bitcast_select_fusion
  253.4 2.0 collective-permute-start.20
  256.9 2.4 collective-permute-start.21
  260.9 6.3 %all-to-all-done.1 = bf16[8,48,1536]{2,1,0:T(8,128)(2,1)} async-done(((bf16[8,48,1536]{2,1,0:T(8,128)(2,1)}), bf16[8,48,1536]{2,1,0:T(8,128)(2,1)}, u32[]{:S(2)}, u32[]{:S(2)}) %all-to-all-start.1) | async-done | bytes 1179680 | tf_op jit(solution)/shard_map/all_to_all | solution.py:204
  267.2 2.6 fusion.126
  270.3 2.5 fusion.127
  272.8 2.7 fusion.13
  275.5 4.5 %all-to-all-start.4 = ((bf16[8,48,1536]{2,1,0:T(8,128)(2,1)}), bf16[8,48,1536]{2,1,0:T(8,128)(2,1)S(1)}, u32[]{:S(2)}, u32[]{:S(2)}) async-start(bf16[8,48,1536]{2,1,0:T(8,128)(2,1)} %bitcast.51), calls=%async_computation.4 | async-start | bytes 2359296 | tf_op jit(solution)/shard_map/all_to_all | solution.py:215
  281.9 14.6 %all-to-all-done.4 = bf16[8,48,1536]{2,1,0:T(8,128)(2,1)S(1)} async-done(((bf16[8,48,1536]{2,1,0:T(8,128)(2,1)}), bf16[8,48,1536]{2,1,0:T(8,128)(2,1)S(1)}, u32[]{:S(2)}, u32[]{:S(2)}) %all-to-all-start.4) | async-done | bytes 1179680 | tf_op jit(solution)/shard_map/all_to_all | solution.py:215
  (165 shorter events, 47.1 us)
Async XLA Ops:
  7.2 22.3 %copy-start.24 = (s32[128,2]{0,1:T(2,128)S(1)}, s32[128,2]{0,1:T(2,128)}, u32[]{:S(2)}) copy-start(s32[128,2]{0,1:T(2,128)} %param.20) | copy-start | bytes 3076
  7.2 23.0 %copy-start.27 = (s32[1,128]{1,0:T(1,128)S(1)}, s32[1,128]{1,0:T(1,128)}, u32[]{:S(2)}) copy-start(s32[1,128]{1,0:T(1,128)} %param.25) | copy-start | bytes 1540
  7.2 25.3 %copy-start.2 = (bf16[1536,256]{1,0:T(8,128)(2,1)S(1)}, bf16[1536,256]{1,0:T(8,128)(2,1)}, u32[]{:S(2)}) copy-start(bf16[1536,256]{1,0:T(8,128)(2,1)} %param.22) | copy-start | bytes 2359300
  7.2 221.2 %all-gather.2.cloned.1.call-start = ((), (), s32[]{:S(2)}) async-start(), calls=%async_computation.5 | async-start | bytes 3538944 | tf_op jit(solution)/shard_map/all_gather | solution.py:165
  10.4 97.3 %collective-permute-start = (bf16[128,1536]{1,0:T(8,128)(2,1)}, bf16[128,1536]{1,0:T(8,128)(2,1)}, u32[]{:S(2)}, u32[]{:S(2)}) collective-permute-start(bf16[128,1536]{1,0:T(8,128)(2,1)} %fusion.27), channel_id=1, source_target_pairs={{0,6},{1,7},{2,0},{3,1},{4,2},{5,3},{6,4},{7,5},{8,14},{9,15},{10,... | collective-permute-start | bytes 1179656 | tf_op jit(solution)/shard_map/ppermute | solution.py:23
  15.6 98.2 %collective-permute-start.1 = (bf16[128,1536]{1,0:T(8,128)(2,1)}, bf16[128,1536]{1,0:T(8,128)(2,1)}, u32[]{:S(2)}, u32[]{:S(2)}) collective-permute-start(bf16[128,1536]{1,0:T(8,128)(2,1)} %fusion.27), channel_id=1, source_target_pairs={{0,4},{1,5},{2,6},{3,7},{4,0},{5,1},{6,2},{7,3},{8,12},{9,13},{10,... | collective-permute-start | bytes 1179656 | tf_op jit(solution)/shard_map/ppermute | solution.py:23
  18.0 20.3 %collective-permute-start.12 = (s32[128]{0:T(128)}, s32[128]{0:T(128)}, u32[]{:S(2)}, u32[]{:S(2)}) collective-permute-start(s32[128]{0:T(128)} %param.19), channel_id=1, source_target_pairs={{0,6},{1,7},{2,0},{3,1},{4,2},{5,3},{6,4},{7,5},{8,14},{9,15},{10,... | collective-permute-start | bytes 1544 | tf_op jit(solution)/shard_map/ppermute | solution.py:23
  20.6 19.7 %collective-permute-start.13 = (s32[128]{0:T(128)}, s32[128]{0:T(128)}, u32[]{:S(2)}, u32[]{:S(2)}) collective-permute-start(s32[128]{0:T(128)} %param.19), channel_id=1, source_target_pairs={{0,4},{1,5},{2,6},{3,7},{4,0},{5,1},{6,2},{7,3},{8,12},{9,13},{10,... | collective-permute-start | bytes 1544 | tf_op jit(solution)/shard_map/ppermute | solution.py:23
  24.3 31.6 %collective-permute-start.14 = (s32[128]{0:T(128)}, s32[128]{0:T(128)}, u32[]{:S(2)}, u32[]{:S(2)}) collective-permute-start(s32[128]{0:T(128)} %param.19), channel_id=1, source_target_pairs={{0,2},{1,3},{2,4},{3,5},{4,6},{5,7},{6,0},{7,1},{8,10},{9,11},{10,... | collective-permute-start | bytes 1544 | tf_op jit(solution)/shard_map/ppermute | solution.py:23
  31.1 4.9 %copy-start.3 = (bf16[1536,256]{1,0:T(8,128)(2,1)S(1)}, bf16[1536,256]{1,0:T(8,128)(2,1)}, u32[]{:S(2)}) copy-start(bf16[1536,256]{1,0:T(8,128)(2,1)} %param.23) | copy-start | bytes 2359300
  36.1 57.3 %copy-start.1 = (bf16[1536,512]{1,0:T(8,128)(2,1)}, bf16[1536,512]{1,0:T(8,128)(2,1)S(1)}, u32[]{:S(2)}) copy-start(bf16[1536,512]{1,0:T(8,128)(2,1)S(1)} %constant_dynamic-update-slice_fusion) | copy-start | bytes 4718596
  38.4 92.1 %collective-permute-start.2 = (bf16[128,1536]{1,0:T(8,128)(2,1)}, bf16[128,1536]{1,0:T(8,128)(2,1)}, u32[]{:S(2)}, u32[]{:S(2)}) collective-permute-start(bf16[128,1536]{1,0:T(8,128)(2,1)} %fusion.27), channel_id=1, source_target_pairs={{0,2},{1,3},{2,4},{3,5},{4,6},{5,7},{6,0},{7,1},{8,10},{9,11},{10,... | collective-permute-start | bytes 1179656 | tf_op jit(solution)/shard_map/ppermute | solution.py:23
  40.3 27.9 %collective-permute-start.3 = (bf16[48,1536]{1,0:T(8,128)(2,1)}, bf16[48,1536]{1,0:T(8,128)(2,1)S(1)}, u32[]{:S(2)}, u32[]{:S(2)}) collective-permute-start(bf16[48,1536]{1,0:T(8,128)(2,1)} %fusion.51), channel_id=1, source_target_pairs={{0,8},{1,9},{2,10},{3,11},{4,12},{5,13},{6,14},{7,15},{8,0},{9,1},... | collective-permute-start | bytes 442376 | tf_op jit(solution)/shard_map/ppermute | solution.py:23
  56.6 7.3 %collective-permute-start.15 = (s32[4,128]{1,0:T(4,128)S(1)}, s32[4,128]{1,0:T(4,128)S(1)}, u32[]{:S(2)}, u32[]{:S(2)}) collective-permute-start(s32[4,128]{1,0:T(4,128)S(1)} %get-tuple-element.19), channel_id=1, source_target_pairs={{0,1},{1,0},{2,3},{3,2},{4,5},{5,4},{6,7},{7,6},{8,9},{9,8},{10,11... | collective-permute-start | bytes 6152 | tf_op jit(solution)/shard_map/ppermute | solution.py:23
  64.0 68.6 %collective-permute-start.7 = (bf16[128,1536]{1,0:T(8,128)(2,1)}, bf16[128,1536]{1,0:T(8,128)(2,1)}, u32[]{:S(2)}, u32[]{:S(2)}) collective-permute-start(bf16[128,1536]{1,0:T(8,128)(2,1)} %pad_maximum_fusion.2), channel_id=1, source_target_pairs={{0,1},{1,0},{2,3},{3,2},{4,5},{5,4},{6,7},{7,6},{8,9},{9,8},{10,11... | collective-permute-start | bytes 1179656 | tf_op jit(solution)/shard_map/ppermute | solution.py:23
  68.3 7.3 %collective-permute-start.4 = (bf16[48,1536]{1,0:T(8,128)(2,1)S(1)}, bf16[48,1536]{1,0:T(8,128)(2,1)S(1)}, u32[]{:S(2)}, u32[]{:S(2)}) collective-permute-start(bf16[48,1536]{1,0:T(8,128)(2,1)S(1)} %collective-permute-done.3), channel_id=1, source_target_pairs={{0,384},{1,385},{2,386},{3,387},{4,388},{5,389},{6,390},{7,391},{8... | collective-permute-start | bytes 442376 | tf_op jit(solution)/shard_map/ppermute | solution.py:23
  75.6 7.4 %collective-permute-start.5 = (bf16[48,1536]{1,0:T(8,128)(2,1)S(1)}, bf16[48,1536]{1,0:T(8,128)(2,1)S(1)}, u32[]{:S(2)}, u32[]{:S(2)}) collective-permute-start(bf16[48,1536]{1,0:T(8,128)(2,1)S(1)} %collective-permute-done.3), channel_id=1, source_target_pairs={{0,256},{1,257},{2,258},{3,259},{4,260},{5,261},{6,262},{7,263},{8... | collective-permute-start | bytes 442376 | tf_op jit(solution)/shard_map/ppermute | solution.py:23
  83.0 7.8 %collective-permute-start.6 = (bf16[48,1536]{1,0:T(8,128)(2,1)S(1)}, bf16[48,1536]{1,0:T(8,128)(2,1)S(1)}, u32[]{:S(2)}, u32[]{:S(2)}) collective-permute-start(bf16[48,1536]{1,0:T(8,128)(2,1)S(1)} %collective-permute-done.3), channel_id=1, source_target_pairs={{0,128},{1,129},{2,130},{3,131},{4,132},{5,133},{6,134},{7,135},{8... | collective-permute-start | bytes 442376 | tf_op jit(solution)/shard_map/ppermute | solution.py:23
  85.9 7.6 %copy-start.14 = (bf16[64,1536]{1,0:T(8,128)(2,1)S(1)}, bf16[64,1536]{1,0:T(8,128)(2,1)}, u32[]{:S(2)}) copy-start(bf16[64,1536]{1,0:T(8,128)(2,1)} %param.18) | copy-start | bytes 589828
  90.8 14.5 %collective-permute-start.18 = (bf16[32,1536]{1,0:T(8,128)(2,1)}, bf16[32,1536]{1,0:T(8,128)(2,1)}, u32[]{:S(2)}, u32[]{:S(2)}) collective-permute-start(bf16[32,1536]{1,0:T(8,128)(2,1)} %constant_dynamic-slice_fusion), channel_id=1, source_target_pairs={{0,8},{1,9},{2,10},{3,11},{4,12},{5,13},{6,14},{7,15},{8,0},{9,1},... | collective-permute-start | bytes 294920 | tf_op jit(solution)/shard_map/ppermute | solution.py:23
  105.3 100.2 %collective-permute-start.16 = (bf16[192,512]{1,0:T(8,128)(2,1)}, bf16[192,512]{1,0:T(8,128)(2,1)}, u32[]{:S(2)}, u32[]{:S(2)}) collective-permute-start(bf16[192,512]{1,0:T(8,128)(2,1)} %constant_dynamic-slice_fusion.1), channel_id=1, source_target_pairs={{0,8},{1,9},{2,10},{3,11},{4,12},{5,13},{6,14},{7,15},{8,0},{9,1},... | collective-permute-start | bytes 589832 | tf_op jit(solution)/shard_map/ppermute | solution.py:23
  107.7 70.7 %collective-permute-start.19 = (bf16[32,1536]{1,0:T(8,128)(2,1)}, bf16[32,1536]{1,0:T(8,128)(2,1)}, u32[]{:S(2)}, u32[]{:S(2)}) collective-permute-start(bf16[32,1536]{1,0:T(8,128)(2,1)} %collective-permute-done.18), channel_id=1, source_target_pairs={{0,16},{1,17},{2,18},{3,19},{4,20},{5,21},{6,22},{7,23},{8,24},{9,... | collective-permute-start | bytes 294920 | tf_op jit(solution)/shard_map/ppermute | solution.py:23
  113.8 20.5 %collective-permute-start.8 = (bf16[128,1536]{1,0:T(8,128)(2,1)S(1)}, bf16[128,1536]{1,0:T(8,128)(2,1)S(1)}, u32[]{:S(2)}, u32[]{:S(2)}) collective-permute-start(bf16[128,1536]{1,0:T(8,128)(2,1)S(1)} %slice.124), channel_id=1, source_target_pairs={{0,1},{1,0},{2,3},{3,2},{4,5},{5,4},{6,7},{7,6},{8,9},{9,8},{10,11... | collective-permute-start | bytes 1179656 | tf_op jit(solution)/shard_map/ppermute | solution.py:23
  134.9 3.4 %collective-permute-start.9 = (bf16[512,256]{0,1:T(8,128)(2,1)S(1)}, bf16[512,256]{0,1:T(8,128)(2,1)S(1)}, u32[]{:S(2)}, u32[]{:S(2)}) collective-permute-start(bf16[512,256]{0,1:T(8,128)(2,1)S(1)} %pad_maximum_fusion.5), channel_id=1, source_target_pairs={{0,1},{1,0},{2,3},{3,2},{4,5},{5,4},{6,7},{7,6},{8,9},{9,8},{10,11... | collective-permute-start | bytes 786440 | tf_op jit(solution)/shard_map/ppermute | solution.py:23
  141.7 47.3 %copy-start.17 = (bf16[1,1024,64]{1,2,0:T(8,128)(2,1)}, bf16[1,1024,64]{1,2,0:T(8,128)(2,1)S(1)}, u32[]{:S(2)}) copy-start(bf16[1,1024,64]{1,2,0:T(8,128)(2,1)S(1)} %get-tuple-element.8) | copy-start | bytes 393220
  141.8 24.7 %collective-permute-start.10 = (bf16[1024,128]{0,1:T(8,128)(2,1)S(1)}, bf16[1024,128]{0,1:T(8,128)(2,1)S(1)}, u32[]{:S(2)}, u32[]{:S(2)}) collective-permute-start(bf16[1024,128]{0,1:T(8,128)(2,1)S(1)} %get-tuple-element.15), channel_id=1, source_target_pairs={{0,8},{1,9},{2,10},{3,11},{4,12},{5,13},{6,14},{7,15},{8,0},{9,1},... | collective-permute-start | bytes 786440 | tf_op jit(solution)/shard_map/ppermute | solution.py:23
  166.5 18.8 %collective-permute-start.11 = (bf16[1024,128]{0,1:T(8,128)(2,1)S(1)}, bf16[1024,128]{0,1:T(8,128)(2,1)S(1)}, u32[]{:S(2)}, u32[]{:S(2)}) collective-permute-start(bf16[1024,128]{0,1:T(8,128)(2,1)S(1)} %collective-permute-done.10), channel_id=1, source_target_pairs={{0,16},{1,17},{2,18},{3,19},{4,20},{5,21},{6,22},{7,23},{16,32},{1... | collective-permute-start | bytes 786440 | tf_op jit(solution)/shard_map/ppermute | solution.py:23
  180.5 20.7 %all-to-all-start.3 = ((bf16[4,64,1536]{2,1,0:T(8,128)(2,1)}), bf16[4,64,1536]{2,1,0:T(8,128)(2,1)S(1)}, u32[]{:S(2)}, u32[]{:S(2)}) async-start(bf16[4,64,1536]{2,1,0:T(8,128)(2,1)} %stack.138), calls=%async_computation.3 | async-start | bytes 1572864 | tf_op jit(solution)/shard_map/all_to_all | solution.py:182
  185.3 3.7 %copy-start.13 = (pred[512,1536]{1,0:T(8,128)(4,1)S(1)}, pred[512,1536]{1,0:T(8,128)(4,1)}, u32[]{:S(2)}) copy-start(pred[512,1536]{1,0:T(8,128)(4,1)} %fusion.8) | copy-start | bytes 2359300
  191.4 3.8 %copy-start.18 = (bf16[1,1024,64]{1,2,0:T(8,128)(2,1)S(1)}, bf16[1,1024,64]{1,2,0:T(8,128)(2,1)}, u32[]{:S(2)}) copy-start(bf16[1,1024,64]{1,2,0:T(8,128)(2,1)} %copy-done.17) | copy-start | bytes 393220
  199.2 5.9 %copy-start.22 = (s32[256]{0:T(256)S(1)}, s32[256]{0:T(256)}, u32[]{:S(2)}) copy-start(s32[256]{0:T(256)} %eq.103) | copy-start | bytes 3076
  199.2 5.9 %copy-start.23 = (s32[8,2]{0,1:T(2,128)S(1)}, s32[8,2]{0,1:T(2,128)}, u32[]{:S(2)}) copy-start(s32[8,2]{0,1:T(2,128)} %slice.112) | copy-start | bytes 196
  199.2 6.1 %copy-start.26 = (pred[128,2]{0,1:T(4,128)(4,1)S(1)}, pred[128,2]{0,1:T(4,128)(4,1)}, u32[]{:S(2)}) copy-start(pred[128,2]{0,1:T(4,128)(4,1)} %broadcast_compare_fusion) | copy-start | bytes 772
  199.2 8.6 %copy-start.11 = (s32[128,2]{1,0:T(8,128)S(1)}, s32[128,2]{1,0:T(8,128)}, u32[]{:S(2)}) copy-start(s32[128,2]{1,0:T(8,128)} %copy-done.10) | copy-start | bytes 3076
  201.1 15.4 %copy-start.6 = (bf16[4,64,1536]{2,1,0:T(8,128)(2,1)}, bf16[4,64,1536]{2,1,0:T(8,128)(2,1)S(1)}, u32[]{:S(2)}) copy-start(bf16[4,64,1536]{2,1,0:T(8,128)(2,1)S(1)} %all-to-all-done.3) | copy-start | bytes 2359300
  201.1 14.1 %all-to-all-start = ((bf16[8,256,128]{2,1,0:T(8,128)(2,1)}), bf16[8,256,128]{2,1,0:T(8,128)(2,1)S(1)}, u32[]{:S(2)}, u32[]{:S(2)}) async-start(bf16[8,256,128]{2,1,0:T(8,128)(2,1)} %pad_maximum_fusion.1), calls=%async_computation | async-start | bytes 1048576 | tf_op jit(solution)/shard_map/all_to_all | solution.py:160
  205.5 8.6 %collective-permute-start.17 = (bf16[192,512]{1,0:T(8,128)(2,1)}, bf16[192,512]{1,0:T(8,128)(2,1)S(1)}, u32[]{:S(2)}, u32[]{:S(2)}) collective-permute-start(bf16[192,512]{1,0:T(8,128)(2,1)} %collective-permute-done.16), channel_id=1, source_target_pairs={{0,16},{1,17},{2,18},{3,19},{4,20},{5,21},{6,22},{7,23},{8,24},{9,... | collective-permute-start | bytes 589832 | tf_op jit(solution)/shard_map/ppermute | solution.py:23
  216.6 27.6 %all-to-all-start.2 = ((bf16[4,384,512]{2,1,0:T(8,128)(2,1)}), bf16[4,384,512]{2,1,0:T(8,128)(2,1)S(1)}, u32[]{:S(2)}, u32[]{:S(2)}) async-start(bf16[4,384,512]{2,1,0:T(8,128)(2,1)} %stack.137), calls=%async_computation.2 | async-start | bytes 3145728 | tf_op jit(solution)/shard_map/all_to_all | solution.py:182
  224.7 3.7 %copy-start = (bf16[128,1536]{1,0:T(8,128)(2,1)S(1)}, bf16[128,1536]{1,0:T(8,128)(2,1)}, u32[]{:S(2)}) copy-start(bf16[128,1536]{1,0:T(8,128)(2,1)} %param.13) | copy-start | bytes 1179652
  244.2 23.0 %all-to-all-start.1 = ((bf16[8,48,1536]{2,1,0:T(8,128)(2,1)}), bf16[8,48,1536]{2,1,0:T(8,128)(2,1)}, u32[]{:S(2)}, u32[]{:S(2)}) async-start(bf16[8,48,1536]{2,1,0:T(8,128)(2,1)} %bitcast.44), calls=%async_computation.1 | async-start | bytes 2359296 | tf_op jit(solution)/shard_map/all_to_all | solution.py:204
  250.6 4.9 %copy-start.7 = (bf16[4,64,1536]{2,1,0:T(8,128)(2,1)S(1)}, bf16[4,64,1536]{2,1,0:T(8,128)(2,1)}, u32[]{:S(2)}) copy-start(bf16[4,64,1536]{2,1,0:T(8,128)(2,1)} %copy-done.6) | copy-start | bytes 2359300
  250.6 4.9 %copy-start.12 = (bf16[256,1536]{1,0:T(8,128)(2,1)S(1)}, bf16[256,1536]{1,0:T(8,128)(2,1)}, u32[]{:S(2)}) copy-start(bf16[256,1536]{1,0:T(8,128)(2,1)} %param.24) | copy-start | bytes 2359300
  253.4 5.9 %copy-start.4 = (bf16[1536,256]{1,0:T(8,128)(2,1)S(1)}, bf16[1536,256]{1,0:T(8,128)(2,1)}, u32[]{:S(2)}) copy-start(bf16[1536,256]{1,0:T(8,128)(2,1)} %param.23) | copy-start | bytes 2359300
  253.4 16.9 %collective-permute-start.20 = (bf16[1536,512]{1,0:T(8,128)(2,1)}, bf16[1536,512]{1,0:T(8,128)(2,1)}, u32[]{:S(2)}, u32[]{:S(2)}) collective-permute-start(bf16[1536,512]{1,0:T(8,128)(2,1)} %bitcast_select_fusion), channel_id=1, source_target_pairs={{0,1},{1,0},{2,3},{3,2},{4,5},{5,4},{6,7},{7,6},{8,9},{9,8},{10,11... | collective-permute-start | bytes 4718600 | tf_op jit(solution)/shard_map/ppermute | solution.py:23
  256.9 16.0 %collective-permute-start.21 = (bf16[256,1536]{1,0:T(8,128)(2,1)}, bf16[256,1536]{1,0:T(8,128)(2,1)}, u32[]{:S(2)}, u32[]{:S(2)}) collective-permute-start(bf16[256,1536]{1,0:T(8,128)(2,1)} %get-tuple-element.4), channel_id=1, source_target_pairs={{0,1},{1,0},{2,3},{3,2},{4,5},{5,4},{6,7},{7,6},{8,9},{9,8},{10,11... | collective-permute-start | bytes 2359304 | tf_op jit(solution)/shard_map/ppermute | solution.py:23
  275.5 4.5 %copy-start.25 = (f32[128,2]{0,1:T(2,128)S(1)}, f32[128,2]{0,1:T(2,128)}, u32[]{:S(2)}) copy-start(f32[128,2]{0,1:T(2,128)} %param.21) | copy-start | bytes 3076
  275.5 4.5 %copy-start.9 = (bf16[8,128,128]{2,1,0:T(8,128)(2,1)S(1)}, bf16[8,128,128]{2,1,0:T(8,128)(2,1)}, u32[]{:S(2)}) copy-start(bf16[8,128,128]{2,1,0:T(8,128)(2,1)} %get-tuple-element.6) | copy-start | bytes 786436
  275.5 21.0 %all-to-all-start.4 = ((bf16[8,48,1536]{2,1,0:T(8,128)(2,1)}), bf16[8,48,1536]{2,1,0:T(8,128)(2,1)S(1)}, u32[]{:S(2)}, u32[]{:S(2)}) async-start(bf16[8,48,1536]{2,1,0:T(8,128)(2,1)} %bitcast.51), calls=%async_computation.4 | async-start | bytes 2359296 | tf_op jit(solution)/shard_map/all_to_all | solution.py:215
  (8 other events, 21.7 us)
Sparse Core Ops, SparseCore 0:
  94.5 42.0 all-gather.1
